TPU v7x, 32 devices: a whole 2x2x4 slice. The times are simulated.
32 devices in a mesh: space: 8 (over z, x), lag: 4 (over y, core).
Axes of the slice: x: 2, y: 2, z: 4, core: 2. Of those that a mesh axis runs over, the one named last changes fastest.
Arguments:
- prior: bfloat16 [8, 4, 64, 1024], P('lag', None, None, 'space'), may hold values from -6 to 6
- obs_value: float32 [8192], P('space'), may hold values from -6 to 6
- obs_weight: float32 [8192], P('space'), may hold values from 0.5 to 4
- obs_coef: float32 [4, 8192], P(None, 'space'), may hold values from 0.1 to 1
- obs_column: int32 [8192], P('space'), may hold values from 0 to 127
- obs_count: int32 [8], P('space'), may hold values from 512 to 1024
- halo_lists: int32 [2, 4096], P(None, 'space'), may hold values from 0 to 1023
- neighbours: int32 [64, 1024], P(None, 'space'), may hold values from 0 to 2047
- localization: float32 [64, 1024], P(None, 'space'), may hold values from 0.05 to 1
Outputs:
- analysis: bfloat16 [8, 4, 64, 1024], P('lag', None, None, 'space')
Inputs may be any that keep to these rules, and one draw needn't show every extreme that they name: `obs_column`: each observation's column within its own tile. `obs_count`: slots at or beyond a tile's count hold no observation. `halo_lists`: slot numbers within the sending tile. `neighbours`: positions in the extended list of the column's tile.
All inputs are finite; a program needn't handle non-finite values.
Results may differ from a plain program's by a relative error of at most 0.0062.
Values may be sent and summed in bfloat16 or wider, within the bound.
A program may use at most 64 MiB of HBM per device.

v0:
```python
import jax
import jax.numpy as jnp
from jax import lax
from jax.sharding import PartitionSpec as P

NSI = 2


def spread(block, axis, holder):
    block = jnp.where(lax.axis_index(axis) == holder, block, jnp.zeros_like(block))
    return lax.psum(block, axis)


def from_behind(value, axis, by):
    length = lax.axis_size(axis)
    pairs = [(i, i + by) for i in range(length) if 0 <= i + by < length]
    return lax.ppermute(value, axis, pairs)


def matmul(left, right):
    return jnp.einsum("ikc,kjc->ijc", left, right, precision=lax.Precision.HIGHEST)


def observe(newest, coef, column, value, weight, count):
    picked = jnp.take(newest, column, axis=2).astype(jnp.float32)
    hx = jnp.sum(coef[:, None, :] * picked, axis=0)
    mean_hx = jnp.mean(hx, axis=0)
    valid = (jnp.arange(column.shape[0]) < count).astype(jnp.float32)
    pert = ((hx - mean_hx[None, :]) * valid[None, :]).astype(jnp.bfloat16)
    info = jnp.stack([weight * valid, (value - mean_hx) * valid]).astype(jnp.bfloat16)
    return (pert, info)


def solve(ext_pert, ext_info, table, local_weight):
    members = ext_pert.shape[0]
    gathered = jnp.take(ext_pert, table, axis=1)
    ginfo = jnp.take(ext_info, table, axis=1)
    weighted = (
        gathered.astype(jnp.float32) * (local_weight * ginfo[0].astype(jnp.float32))[None]
    ).astype(jnp.bfloat16)
    gram = jnp.einsum("inc,jnc->ijc", gathered, weighted, preferred_element_type=jnp.float32)
    drive = jnp.einsum("inc,nc->ic", weighted, ginfo[1], preferred_element_type=jnp.float32)
    eye = jnp.eye(members, dtype=jnp.float32)[:, :, None]
    matrix = eye + gram / (members - 1)
    scale = jnp.sqrt(jnp.sum(matrix * matrix, axis=(0, 1)))
    ycur = matrix / scale[None, None, :]
    zcur = jnp.broadcast_to(eye, matrix.shape)
    for step in range(NSI):
        smat = 1.5 * eye - 0.5 * matmul(zcur, ycur)
        ycur = matmul(ycur, smat)
        zcur = matmul(smat, zcur)
    inverse = matmul(zcur, zcur) / scale[None, None, :]
    mean_weight = jnp.einsum("ijc,jc->ic", inverse, drive, precision=lax.Precision.HIGHEST) / (
        members - 1
    )
    root = zcur / jnp.sqrt(scale)[None, None, :]
    return (root + mean_weight[:, None, :]).astype(jnp.bfloat16)


def body(
    prior,
    obs_value,
    obs_weight,
    obs_coef,
    obs_column,
    obs_count,
    halo_lists,
    neighbours,
    localization,
):
    lags = lax.axis_size("lag")
    newest = spread(prior[-1], "lag", lags - 1)
    pert, info = observe(newest, obs_coef, obs_column, obs_value, obs_weight, obs_count[0])
    upward = (jnp.take(pert, halo_lists[0], axis=1), jnp.take(info, halo_lists[0], axis=1))
    downward = (jnp.take(pert, halo_lists[1], axis=1), jnp.take(info, halo_lists[1], axis=1))
    below_pert, below_info = from_behind((upward[0], upward[1]), "space", 1)
    above_pert, above_info = from_behind((downward[0], downward[1]), "space", -1)
    ext_pert = jnp.concatenate([pert, below_pert, above_pert], axis=1)
    ext_info = jnp.concatenate([info, below_info, above_info], axis=1)
    share = neighbours.shape[1] // lags
    start = lax.axis_index("lag") * share
    table = lax.dynamic_slice_in_dim(neighbours, start, share, 1)
    local_weight = lax.dynamic_slice_in_dim(localization, start, share, 1)
    portion = solve(ext_pert, ext_info, table, local_weight)
    trans = lax.all_gather(portion, "lag", axis=2, tiled=True)
    values = prior.astype(jnp.float32)
    prior_mean = jnp.mean(values, axis=2, keepdims=True)
    prior_pert = (values - prior_mean).astype(jnp.bfloat16)
    mixed = jnp.einsum("lskc,kjc->lsjc", prior_pert, trans, preferred_element_type=jnp.float32)
    return (prior_mean + mixed).astype(jnp.bfloat16)


def solution(mesh):
    return jax.shard_map(
        body,
        mesh=mesh,
        in_specs=(
            P("lag", None, None, "space"),
            P("space"),
            P("space"),
            P(None, "space"),
            P("space"),
            P("space"),
            P(None, "space"),
            P(None, "space"),
            P(None, "space"),
        ),
        out_specs=P("lag", None, None, "space"),
        check_vma=False,
    )
```

profile of v0, /device:TPU:0, one launch (start us, length us, event | category | flops | bytes accessed | tf_op | source)
XLA Modules:
  0.0 141.3 jit_solution(15085196720965544644)
XLA Ops:
  6.5 0.8 slice.17
  7.4 0.1 copy.101
  7.5 0.7 select_bitcast_fusion.4
  8.3 0.7 compare_and_fusion.1
  9.0 0.7 fusion.24
  9.7 0.8 fusion.27
  11.2 0.8 compare_and_fusion
  12.2 0.7 select_convert_fusion.1
  12.9 0.9 copy.73
  13.9 30.3 %all-reduce.2.cloned.1.call-done = bf16[4,64,128]{1,0,2:T(4,128)(2,1)} async-done(((bf16[4,64,128]{1,0,2:T(4,128)(2,1)}), bf16[4,64,128]{1,0,2:T(4,128)(2,1)}) %all-reduce.2.cloned.1.call-update) | async-done | bytes 65552 | tf_op jit(solution)/shard_map/psum | solution.py:11
  44.2 4.5 %gather_fusion = bf16[1024,4,64]{2,1,0:T(4,128)(2,1)S(1)} fusion(bf16[4,64,128]{1,0,2:T(4,128)(2,1)} %all-reduce.2.cloned.1.call-done, s32[1024]{0:T(1024)S(1)} %fusion.24), kind=kCustom, calls=%fused_computation.4 | custom fusion | bytes 1052672 | tf_op jit(solution)/shard_map/jit(_take)/gather | solution.py:25
  48.7 16.1 %fusion.3 = (f32[64,1024]{0,1:T(8,128)S(1)}, f32[1024]{0:T(1024)S(1)}) fusion(f32[4,1024]{0,1:T(8,128)S(1)} %copy.73, bf16[1024,4,64]{2,1,0:T(4,128)(2,1)S(1)} %gather_fusion, pred[1024]{0:T(1024)(128)(4,1)S(1)} %compare_and_fusion.1), kind=kLoop, calls=%fused_computation.11 | loop fusion | flops 1244160 | bytes 807936 | tf_op jit(solution)/shard_map/reduce_sum | solution.py:26
  64.8 0.3 multiply_convert_fusion.3
  65.2 1.3 gather_fusion.4
  66.5 1.3 gather_fusion.3
  67.9 0.2 copy.78
  68.1 1.3 gather_fusion.6
  69.5 1.3 gather_fusion.5
  70.8 0.1 select_bitcast_fusion.2
  71.0 0.1 select_bitcast_fusion
  71.1 0.1 select_bitcast_fusion.1
  71.2 3.4 %collective-permute-start.2 = (bf16[2,512]{0,1:T(8,128)(2,1)S(1)}, bf16[2,512]{0,1:T(8,128)(2,1)S(1)}, u32[]{:S(2)}, u32[]{:S(2)}) collective-permute-start(bf16[2,512]{0,1:T(8,128)(2,1)S(1)} %select_bitcast_fusion.1), channel_id=1, source_target_pairs={{0,4},{4,8},{8,12},{12,16},{16,20},{20,24},{24,28},{1,5},{5,9},{9,... | collective-permute-start | bytes 6152 | tf_op jit(solution)/shard_map/ppermute | solution.py:17
  74.6 1.3 collective-permute-start.3
  75.9 0.1 select_bitcast_fusion.3
  76.1 4.6 %collective-permute-start = (bf16[64,512]{0,1:T(8,128)(2,1)S(1)}, bf16[64,512]{0,1:T(8,128)(2,1)S(1)}, u32[]{:S(2)}, u32[]{:S(2)}) collective-permute-start(bf16[64,512]{0,1:T(8,128)(2,1)S(1)} %select_bitcast_fusion.3), channel_id=1, source_target_pairs={{0,4},{4,8},{8,12},{12,16},{16,20},{20,24},{24,28},{1,5},{5,9},{9,... | collective-permute-start | bytes 196616 | tf_op jit(solution)/shard_map/ppermute | solution.py:17
  80.6 1.5 %collective-permute-start.1 = (bf16[64,512]{0,1:T(8,128)(2,1)S(1)}, bf16[64,512]{0,1:T(8,128)(2,1)S(1)}, u32[]{:S(2)}, u32[]{:S(2)}) collective-permute-start(bf16[64,512]{0,1:T(8,128)(2,1)S(1)} %select_bitcast_fusion.2), channel_id=1, source_target_pairs={{4,0},{8,4},{12,8},{16,12},{20,16},{24,20},{28,24},{5,1},{9,5},{13... | collective-permute-start | bytes 196616 | tf_op jit(solution)/shard_map/ppermute | solution.py:17
  82.1 0.1 pad_maximum_fusion.1
  82.2 6.2 %gather_fusion.2 = bf16[2048,2]{1,0:T(8,128)(2,1)S(1)} fusion(bf16[2,2048]{0,1:T(8,128)(2,1)S(1)} %pad_maximum_fusion.1, s32[2048]{0:T(1024)S(1)} %broadcast_clamp_fusion), kind=kCustom, calls=%fused_computation.6 | custom fusion | bytes 24576 | tf_op jit(solution)/shard_map/jit(_take)/gather | solution.py:37
  88.4 0.5 copy.79
  89.2 0.1 pad_maximum_fusion
  89.3 6.2 %gather_fusion.1 = bf16[2048,64]{1,0:T(8,128)(2,1)S(1)} fusion(bf16[64,2048]{0,1:T(8,128)(2,1)S(1)} %pad_maximum_fusion, s32[2048]{0:T(1024)S(1)} %broadcast_clamp_fusion), kind=kCustom, calls=%fused_computation.5 | custom fusion | bytes 532480 | tf_op jit(solution)/shard_map/jit(_take)/gather | solution.py:36
  95.5 0.6 copy.75
  96.1 0.5 multiply_reduce_fusion
  96.7 1.2 fusion.8
  97.9 1.2 convolution_bitcast_fusion.1
  99.1 1.0 convolution_bitcast_fusion.2
  100.2 0.4 convolution_bitcast_fusion.3
  100.6 1.3 fusion.6
  101.8 1.2 convolution_bitcast_fusion
  103.0 1.2 fusion.4
  104.2 1.0 fusion.28
  105.2 0.2 add_convert_fusion
  105.5 1.0 copy.87
  106.6 0.2 copy.88
  106.8 24.5 %all-gather.2.cloned.1.call-done = bf16[64,64,128]{1,0,2:T(8,128)(2,1)} async-done(((bf16[64,64,32]{1,0,2:T(8,128)(2,1)}), bf16[64,64,128]{1,0,2:T(8,128)(2,1)}) %all-gather.2.cloned.1.call-update) | async-done | bytes 1048592 | tf_op jit(solution)/shard_map/all_gather | solution.py:85
  131.3 2.2 %fusion = f32[128,64,2,4]{1,3,2,0:T(4,128)S(1)} fusion(bf16[2,4,64,128]{2,1,0,3:T(4,128)(2,1)S(1)} %copy.88, bf16[64,64,128]{1,0,2:T(8,128)(2,1)} %all-gather.2.cloned.1.call-done), kind=kOutput, calls=%fused_computation.7 | convolution fusion | flops 8388608 | bytes 1441792 | tf_op jit(solution)/shard_map/lskc,kjc->lsjc/dot_general | solution.py:89
  133.5 0.2 copy.89
  133.7 0.7 fusion.18
  (40 shorter events, 0.7 us)
Async XLA Ops:
  6.5 37.7 %all-reduce.2.cloned.1.call-start = ((), (), s32[]{:S(2)}) async-start(), calls=%async_computation | async-start | bytes 262144 | tf_op jit(solution)/shard_map/psum | solution.py:11
  8.2 56.6 %copy-start.2 = (f32[1024]{0:T(1024)S(1)}, f32[1024]{0:T(1024)}, u32[]{:S(2)}) copy-start(f32[1024]{0:T(1024)} %param.14) | copy-start | bytes 12292
  8.3 123.0 %all-gather.2.cloned.1.call-start = ((), (), s32[]{:S(2)}) async-start(), calls=%async_computation.1 | async-start | bytes 2621440 | tf_op jit(solution)/shard_map/all_gather | solution.py:85
  66.5 22.4 %copy-start.1 = (f32[64,128]{1,0:T(8,128)S(1)}, f32[64,128]{1,0:T(8,128)}, u32[]{:S(2)}) copy-start(f32[64,128]{1,0:T(8,128)} %param.21) | copy-start | bytes 98308
  71.2 10.9 %collective-permute-start.2 = (bf16[2,512]{0,1:T(8,128)(2,1)S(1)}, bf16[2,512]{0,1:T(8,128)(2,1)S(1)}, u32[]{:S(2)}, u32[]{:S(2)}) collective-permute-start(bf16[2,512]{0,1:T(8,128)(2,1)S(1)} %select_bitcast_fusion.1), channel_id=1, source_target_pairs={{0,4},{4,8},{8,12},{12,16},{16,20},{20,24},{24,28},{1,5},{5,9},{9,... | collective-permute-start | bytes 6152 | tf_op jit(solution)/shard_map/ppermute | solution.py:17
  74.6 7.5 %collective-permute-start.3 = (bf16[2,512]{0,1:T(8,128)(2,1)S(1)}, bf16[2,512]{0,1:T(8,128)(2,1)S(1)}, u32[]{:S(2)}, u32[]{:S(2)}) collective-permute-start(bf16[2,512]{0,1:T(8,128)(2,1)S(1)} %select_bitcast_fusion), channel_id=1, source_target_pairs={{4,0},{8,4},{12,8},{16,12},{20,16},{24,20},{28,24},{5,1},{9,5},{13... | collective-permute-start | bytes 6152 | tf_op jit(solution)/shard_map/ppermute | solution.py:17
  76.1 13.1 %collective-permute-start = (bf16[64,512]{0,1:T(8,128)(2,1)S(1)}, bf16[64,512]{0,1:T(8,128)(2,1)S(1)}, u32[]{:S(2)}, u32[]{:S(2)}) collective-permute-start(bf16[64,512]{0,1:T(8,128)(2,1)S(1)} %select_bitcast_fusion.3), channel_id=1, source_target_pairs={{0,4},{4,8},{8,12},{12,16},{16,20},{20,24},{24,28},{1,5},{5,9},{9,... | collective-permute-start | bytes 196616 | tf_op jit(solution)/shard_map/ppermute | solution.py:17
  80.6 8.6 %collective-permute-start.1 = (bf16[64,512]{0,1:T(8,128)(2,1)S(1)}, bf16[64,512]{0,1:T(8,128)(2,1)S(1)}, u32[]{:S(2)}, u32[]{:S(2)}) collective-permute-start(bf16[64,512]{0,1:T(8,128)(2,1)S(1)} %select_bitcast_fusion.2), channel_id=1, source_target_pairs={{4,0},{8,4},{12,8},{16,12},{20,16},{24,20},{28,24},{5,1},{9,5},{13... | collective-permute-start | bytes 196616 | tf_op jit(solution)/shard_map/ppermute | solution.py:17
  104.2 2.3 %copy-start = (bf16[2,4,64,128]{3,2,1,0:T(8,128)(2,1)S(1)}, bf16[2,4,64,128]{3,2,1,0:T(8,128)(2,1)}, u32[]{:S(2)}) copy-start(bf16[2,4,64,128]{3,2,1,0:T(8,128)(2,1)} %param.13) | copy-start | bytes 393220
Sparse Core Ops, SparseCore 0:
  9.6 34.4 all-reduce.1
  106.6 24.6 all-gather.1
where the time goes:
time: 142 us; the launch traced here: 141 us
  waiting for transfers between devices  54.8 us (39%)
  local copies, waits for them, and re-layouts  28 us (20%)
  other arithmetic  22.1 us (16%)
  between operations  14.5 us (10%)
  matrix products  11.2 us (8%)
  starting transfers between devices  10.7 us (8%)
    psum x1, waiting for transfers between devices, spread(): return lax.psum(block, axis)  30.3 us
    all_gather x1, waiting for transfers between devices, body(): trans = lax.all_gather(portion, 'lag', axis=2, tiled=True)  24.5 us
    reduce_sum x1, other arithmetic, observe(): hx = jnp.sum(coef[:, None, :] * picked, axis=0)  16.1 us
    ppermute x4, starting transfers between devices, from_behind(): return lax.ppermute(value, axis, pairs)  10.7 us
    dot_general x6, matrix products, matmul(): jnp.einsum('ikc,kjc->ijc', left, right, precision=lax.Precision.HIGHEST)  7.1 us
    gather x2, local copies, waits for them, and re-layouts, solve(): gathered = jnp.take(ext_pert, table, axis=1)  6.8 us
    gather x2, local copies, waits for them, and re-layouts, solve(): ginfo = jnp.take(ext_info, table, axis=1)  6.67 us
    gather x1, local copies, waits for them, and re-layouts, observe(): picked = jnp.take(newest, column, axis=2).astype(jnp.float32)  4.46 us
  transfers between devices with their start and end apart: 6, of which 2 were waited for; matrix products, arithmetic and copies ran while one was open for 9% of the time, Pallas kernels for 0%

commit v1 on v0

--- a/solution.py
+++ b/solution.py
@@ -8,7 +8,7 @@
 
 def spread(block, axis, holder):
     block = jnp.where(lax.axis_index(axis) == holder, block, jnp.zeros_like(block))
-    return lax.psum(block, axis)
+    return jnp.sum(lax.all_gather(block, axis), axis=0)
 
 
 def from_behind(value, axis, by):

time: 142 us -> 121 us (0.85)
  waiting for transfers between devices: 54.8 us -> 29.6 us
  blocking collectives: 0 us -> 7.23 us
  local copies, waits for them, and re-layouts: 28 us -> 26.3 us
    psum x1 -> x0, waiting for transfers between devices: 30.3 us -> none  [spread(): return lax.psum(block, axis)]
    all_gather x0 -> x1, blocking collectives: none -> 7.23 us  [spread(): return jnp.sum(lax.all_gather(block, axis), axis=0)]
    ppermute x4, waiting for transfers between devices: 0.01 us -> 5.74 us  [from_behind(): return lax.ppermute(value, axis, pairs)]
  transfers between devices with their start and end apart: 6 -> 5, of which waited for: 2 -> 2; matrix products, arithmetic and copies ran while one was open for 9% -> 10% of each run, Pallas kernels for 0% -> 0%
where the time goes in v1:
time: 121 us; the launch traced here: 120 us
  waiting for transfers between devices  29.6 us (24%)
  local copies, waits for them, and re-layouts  26.3 us (22%)
  other arithmetic  20.8 us (17%)
  between operations  14.5 us (12%)
  matrix products  11.2 us (9%)
  starting transfers between devices  10.7 us (9%)
  blocking collectives  7.23 us (6%)
    all_gather x1, waiting for transfers between devices, body(): trans = lax.all_gather(portion, 'lag', axis=2, tiled=True)  23.9 us
    reduce_sum x1, other arithmetic, observe(): hx = jnp.sum(coef[:, None, :] * picked, axis=0)  16.1 us
    ppermute x4, starting transfers between devices, from_behind(): return lax.ppermute(value, axis, pairs)  10.7 us
    all_gather x1, blocking collectives, spread(): return jnp.sum(lax.all_gather(block, axis), axis=0)  7.23 us
    dot_general x6, matrix products, matmul(): jnp.einsum('ikc,kjc->ijc', left, right, precision=lax.Precision.HIGHEST)  7.1 us
    gather x2, local copies, waits for them, and re-layouts, solve(): gathered = jnp.take(ext_pert, table, axis=1)  6.8 us
    gather x2, local copies, waits for them, and re-layouts, solve(): ginfo = jnp.take(ext_info, table, axis=1)  6.68 us
    ppermute x4, waiting for transfers between devices, from_behind(): return lax.ppermute(value, axis, pairs)  5.74 us
  transfers between devices with their start and end apart: 5, of which 2 were waited for; matrix products, arithmetic and copies ran while one was open for 10% of the time, Pallas kernels for 0%

profile of v1, /device:TPU:0, one launch (start us, length us, event | category | flops | bytes accessed | tf_op | source)
XLA Modules:
  0.0 120.4 jit_solution(8318158720244415926)
XLA Ops:
  6.5 0.7 compare_and_fusion.1
  7.2 0.7 fusion.24
  7.9 0.8 fusion.27
  9.4 0.9 slice_select_fusion
  10.2 7.2 %all_gather.7 = bf16[4,4,64,128]{3,2,1,0:T(8,128)(2,1)S(1)} all-gather(bf16[1,4,64,128]{3,2,1,0:T(8,128)(2,1)S(1)} %slice_select_fusion), channel_id=1, replica_groups=mesh['space'=8,'lag'=4] {'lag'}, dimensions={0}, use_global_device_ids=true | all-gather | bytes 327680 | tf_op jit(solution)/shard_map/all_gather | solution.py:11
  17.5 0.1 copy.73
  17.7 0.9 copy.72
  18.6 3.6 %gather_fusion = bf16[1024,4,64]{2,1,0:T(4,128)(2,1)S(1)} fusion(bf16[4,64,128]{1,0,2:T(4,128)(2,1)S(1)} %copy.73, s32[1024]{0:T(1024)S(1)} %fusion.24), kind=kCustom, calls=%fused_computation.4 | custom fusion | bytes 1052672 | tf_op jit(solution)/shard_map/jit(_take)/gather | solution.py:25
  22.2 16.1 %fusion.3 = (f32[64,1024]{0,1:T(8,128)S(1)}, f32[1024]{0:T(1024)S(1)}) fusion(f32[4,1024]{0,1:T(8,128)S(1)} %copy.72, bf16[1024,4,64]{2,1,0:T(4,128)(2,1)S(1)} %gather_fusion, pred[1024]{0:T(1024)(128)(4,1)S(1)} %compare_and_fusion.1), kind=kLoop, calls=%fused_computation.11 | loop fusion | flops 1244160 | bytes 807936 | tf_op jit(solution)/shard_map/reduce_sum | solution.py:26
  38.4 0.3 multiply_convert_fusion.3
  38.7 1.3 %gather_fusion.3 = bf16[512,64]{1,0:T(8,128)(2,1)S(1)} fusion(bf16[64,1024]{0,1:T(8,128)(2,1)S(1)} %multiply_convert_fusion.3, s32[1024]{0:T(1024)S(1)} %pad_clamp_fusion.1), kind=kCustom, calls=%fused_computation.clone | custom fusion | bytes 133120 | tf_op jit(solution)/shard_map/jit(_take)/gather | solution.py:74
  40.1 0.1 select_bitcast_fusion.3
  40.2 3.4 %collective-permute-start = (bf16[64,512]{0,1:T(8,128)(2,1)S(1)}, bf16[64,512]{0,1:T(8,128)(2,1)S(1)}, u32[]{:S(2)}, u32[]{:S(2)}) collective-permute-start(bf16[64,512]{0,1:T(8,128)(2,1)S(1)} %select_bitcast_fusion.3), channel_id=1, source_target_pairs={{0,4},{4,8},{8,12},{12,16},{16,20},{20,24},{24,28},{1,5},{5,9},{9,... | collective-permute-start | bytes 196616 | tf_op jit(solution)/shard_map/ppermute | solution.py:17
  43.7 1.3 %gather_fusion.4 = bf16[512,64]{1,0:T(8,128)(2,1)S(1)} fusion(bf16[64,1024]{0,1:T(8,128)(2,1)S(1)} %multiply_convert_fusion.3, s32[1024]{0:T(1024)S(1)} %pad_clamp_fusion), kind=kCustom, calls=%fused_computation.2.clone | custom fusion | bytes 133120 | tf_op jit(solution)/shard_map/jit(_take)/gather | solution.py:75
  45.0 0.1 select_bitcast_fusion.2
  45.2 1.3 %collective-permute-start.1 = (bf16[64,512]{0,1:T(8,128)(2,1)S(1)}, bf16[64,512]{0,1:T(8,128)(2,1)S(1)}, u32[]{:S(2)}, u32[]{:S(2)}) collective-permute-start(bf16[64,512]{0,1:T(8,128)(2,1)S(1)} %select_bitcast_fusion.2), channel_id=1, source_target_pairs={{4,0},{8,4},{12,8},{16,12},{20,16},{24,20},{28,24},{5,1},{9,5},{13... | collective-permute-start | bytes 196616 | tf_op jit(solution)/shard_map/ppermute | solution.py:17
  46.5 0.2 copy.77
  46.7 1.3 %gather_fusion.5 = bf16[512,2]{1,0:T(8,128)(2,1)S(1)} fusion(bf16[2,1024]{0,1:T(8,128)(2,1)S(1)} %copy.77, s32[1024]{0:T(1024)S(1)} %pad_clamp_fusion.1), kind=kCustom, calls=%fused_computation.1.clone | custom fusion | bytes 6144 | tf_op jit(solution)/shard_map/jit(_take)/gather | solution.py:74
  48.1 0.1 select_bitcast_fusion.1
  48.2 4.6 %collective-permute-start.2 = (bf16[2,512]{0,1:T(8,128)(2,1)S(1)}, bf16[2,512]{0,1:T(8,128)(2,1)S(1)}, u32[]{:S(2)}, u32[]{:S(2)}) collective-permute-start(bf16[2,512]{0,1:T(8,128)(2,1)S(1)} %select_bitcast_fusion.1), channel_id=1, source_target_pairs={{0,4},{4,8},{8,12},{12,16},{16,20},{20,24},{24,28},{1,5},{5,9},{9,... | collective-permute-start | bytes 6152 | tf_op jit(solution)/shard_map/ppermute | solution.py:17
  52.8 1.3 %gather_fusion.6 = bf16[512,2]{1,0:T(8,128)(2,1)S(1)} fusion(bf16[2,1024]{0,1:T(8,128)(2,1)S(1)} %copy.77, s32[1024]{0:T(1024)S(1)} %pad_clamp_fusion), kind=kCustom, calls=%fused_computation.3.clone | custom fusion | bytes 6144 | tf_op jit(solution)/shard_map/jit(_take)/gather | solution.py:75
  54.1 0.1 select_bitcast_fusion
  54.3 1.5 %collective-permute-start.3 = (bf16[2,512]{0,1:T(8,128)(2,1)S(1)}, bf16[2,512]{0,1:T(8,128)(2,1)S(1)}, u32[]{:S(2)}, u32[]{:S(2)}) collective-permute-start(bf16[2,512]{0,1:T(8,128)(2,1)S(1)} %select_bitcast_fusion), channel_id=1, source_target_pairs={{4,0},{8,4},{12,8},{16,12},{20,16},{24,20},{28,24},{5,1},{9,5},{13... | collective-permute-start | bytes 6152 | tf_op jit(solution)/shard_map/ppermute | solution.py:17
  55.8 0.1 compare_and_fusion
  56.1 5.7 %collective-permute-done.3 = bf16[2,512]{0,1:T(8,128)(2,1)S(1)} collective-permute-done((bf16[2,512]{0,1:T(8,128)(2,1)S(1)}, bf16[2,512]{0,1:T(8,128)(2,1)S(1)}, u32[]{:S(2)}, u32[]{:S(2)}) %collective-permute-start.3) | collective-permute-done | bytes 2080 | tf_op jit(solution)/shard_map/ppermute | solution.py:17
  61.8 0.1 pad_maximum_fusion.1
  61.9 6.2 %gather_fusion.2 = bf16[2048,2]{1,0:T(8,128)(2,1)S(1)} fusion(bf16[2,2048]{0,1:T(8,128)(2,1)S(1)} %pad_maximum_fusion.1, s32[2048]{0:T(1024)S(1)} %broadcast_clamp_fusion), kind=kCustom, calls=%fused_computation.6 | custom fusion | bytes 24576 | tf_op jit(solution)/shard_map/jit(_take)/gather | solution.py:37
  68.1 0.5 copy.78
  68.8 0.1 copy.94
  68.9 0.1 pad_maximum_fusion
  69.0 6.2 %gather_fusion.1 = bf16[2048,64]{1,0:T(8,128)(2,1)S(1)} fusion(bf16[64,2048]{0,1:T(8,128)(2,1)S(1)} %pad_maximum_fusion, s32[2048]{0:T(1024)S(1)} %broadcast_clamp_fusion), kind=kCustom, calls=%fused_computation.5 | custom fusion | bytes 532480 | tf_op jit(solution)/shard_map/jit(_take)/gather | solution.py:36
  75.2 0.6 copy.74
  75.8 0.5 multiply_reduce_fusion
  76.4 1.2 fusion.8
  77.6 1.2 %convolution_bitcast_fusion.1 = f32[64,64,32]{0,1,2:T(8,128)S(1)} fusion(f32[64,64,32]{0,1,2:T(8,128)S(1)} %fusion.8, f32[64,64,32]{0,1,2:T(8,128)S(1)} %get-tuple-element.18, f32[32]{0:T(128)S(1)} %get-tuple-element.16), kind=kOutput, calls=%fused_computation.18 | convolution fusion | flops 100794368 | bytes 1572992 | tf_op jit(solution)/shard_map/ikc,kjc->ijc/dot_general | solution.py:21
  78.8 1.0 convolution_bitcast_fusion.2
  79.9 0.4 convolution_bitcast_fusion.3
  80.2 1.3 %fusion.6 = f32[64,64,32]{0,1,2:T(8,128)S(1)} fusion(f32[64,64,32]{0,1,2:T(8,128)S(1)} %convolution_bitcast_fusion.1, f32[64,64,32]{0,1,2:T(8,128)S(1)} %convolution_bitcast_fusion.2, f32[64,64]{0,1:T(8,128)S(1)} %fusion.21), kind=kOutput, calls=%fused_computation.17 | convolution fusion | flops 100925440 | bytes 1589248 | tf_op jit(solution)/shard_map/ikc,kjc->ijc/dot_general | solution.py:21
  81.5 1.2 convolution_bitcast_fusion
  82.7 1.2 fusion.4
  83.9 1.0 fusion.28
  84.9 0.2 add_convert_fusion
  85.1 1.0 copy.86
  86.3 0.2 copy.87
  86.5 23.9 %all-gather.2.cloned.1.call-done = bf16[64,64,128]{1,0,2:T(8,128)(2,1)} async-done(((bf16[64,64,32]{1,0,2:T(8,128)(2,1)}), bf16[64,64,128]{1,0,2:T(8,128)(2,1)}) %all-gather.2.cloned.1.call-update) | async-done | bytes 1048592 | tf_op jit(solution)/shard_map/all_gather | solution.py:85
  110.3 2.2 %fusion = f32[128,64,2,4]{1,3,2,0:T(4,128)S(1)} fusion(bf16[2,4,64,128]{2,1,0,3:T(4,128)(2,1)S(1)} %copy.87, bf16[64,64,128]{1,0,2:T(8,128)(2,1)} %all-gather.2.cloned.1.call-done), kind=kOutput, calls=%fused_computation.7 | convolution fusion | flops 8388608 | bytes 1441792 | tf_op jit(solution)/shard_map/lskc,kjc->lsjc/dot_general | solution.py:89
  112.6 0.2 copy.88
  112.8 0.7 fusion.18
  (42 shorter events, 0.6 us)
Async XLA Ops:
  6.5 103.8 %all-gather.2.cloned.1.call-start = ((), (), s32[]{:S(2)}) async-start(), calls=%async_computation | async-start | bytes 2621440 | tf_op jit(solution)/shard_map/all_gather | solution.py:85
  17.5 20.9 %copy-start.4 = (f32[1024]{0:T(1024)S(1)}, f32[1024]{0:T(1024)}, u32[]{:S(2)}) copy-start(f32[1024]{0:T(1024)} %param.14) | copy-start | bytes 12292
  22.2 24.3 %copy-start.3 = (f32[1024]{0:T(1024)S(1)}, f32[1024]{0:T(1024)}, u32[]{:S(2)}) copy-start(f32[1024]{0:T(1024)} %param.15) | copy-start | bytes 12292
  38.4 17.4 %copy-start.1 = (s32[64,128]{1,0:T(8,128)S(1)}, s32[64,128]{1,0:T(8,128)}, u32[]{:S(2)}) copy-start(s32[64,128]{1,0:T(8,128)} %param.20) | copy-start | bytes 98308
  40.1 28.5 %copy-start.2 = (f32[64,128]{1,0:T(8,128)S(1)}, f32[64,128]{1,0:T(8,128)}, u32[]{:S(2)}) copy-start(f32[64,128]{1,0:T(8,128)} %param.21) | copy-start | bytes 98308
  40.2 28.7 %collective-permute-start = (bf16[64,512]{0,1:T(8,128)(2,1)S(1)}, bf16[64,512]{0,1:T(8,128)(2,1)S(1)}, u32[]{:S(2)}, u32[]{:S(2)}) collective-permute-start(bf16[64,512]{0,1:T(8,128)(2,1)S(1)} %select_bitcast_fusion.3), channel_id=1, source_target_pairs={{0,4},{4,8},{8,12},{12,16},{16,20},{20,24},{24,28},{1,5},{5,9},{9,... | collective-permute-start | bytes 196616 | tf_op jit(solution)/shard_map/ppermute | solution.py:17
  45.2 23.7 %collective-permute-start.1 = (bf16[64,512]{0,1:T(8,128)(2,1)S(1)}, bf16[64,512]{0,1:T(8,128)(2,1)S(1)}, u32[]{:S(2)}, u32[]{:S(2)}) collective-permute-start(bf16[64,512]{0,1:T(8,128)(2,1)S(1)} %select_bitcast_fusion.2), channel_id=1, source_target_pairs={{4,0},{8,4},{12,8},{16,12},{20,16},{24,20},{28,24},{5,1},{9,5},{13... | collective-permute-start | bytes 196616 | tf_op jit(solution)/shard_map/ppermute | solution.py:17
  48.2 7.8 %collective-permute-start.2 = (bf16[2,512]{0,1:T(8,128)(2,1)S(1)}, bf16[2,512]{0,1:T(8,128)(2,1)S(1)}, u32[]{:S(2)}, u32[]{:S(2)}) collective-permute-start(bf16[2,512]{0,1:T(8,128)(2,1)S(1)} %select_bitcast_fusion.1), channel_id=1, source_target_pairs={{0,4},{4,8},{8,12},{12,16},{16,20},{20,24},{24,28},{1,5},{5,9},{9,... | collective-permute-start | bytes 6152 | tf_op jit(solution)/shard_map/ppermute | solution.py:17
  54.3 7.5 %collective-permute-start.3 = (bf16[2,512]{0,1:T(8,128)(2,1)S(1)}, bf16[2,512]{0,1:T(8,128)(2,1)S(1)}, u32[]{:S(2)}, u32[]{:S(2)}) collective-permute-start(bf16[2,512]{0,1:T(8,128)(2,1)S(1)} %select_bitcast_fusion), channel_id=1, source_target_pairs={{4,0},{8,4},{12,8},{16,12},{20,16},{24,20},{28,24},{5,1},{9,5},{13... | collective-permute-start | bytes 6152 | tf_op jit(solution)/shard_map/ppermute | solution.py:17
  83.9 2.3 %copy-start = (bf16[2,4,64,128]{3,2,1,0:T(8,128)(2,1)S(1)}, bf16[2,4,64,128]{3,2,1,0:T(8,128)(2,1)}, u32[]{:S(2)}) copy-start(bf16[2,4,64,128]{3,2,1,0:T(8,128)(2,1)} %param.13) | copy-start | bytes 393220
Sparse Core Ops, SparseCore 0:
  86.3 24.0 all-gather.1
